TPU v7x, 128 devices: a whole 4x4x4 slice. The times are simulated.
128 devices in a mesh: rows: 8 (over x, core), cols: 16 (over z, y).
Axes of the slice: x: 4, y: 4, z: 4, core: 2. Of those that a mesh axis runs over, the one named last changes fastest.
Arguments:
- blocks: bfloat16 [96, 96, 256, 256], P('rows', 'cols'), may hold values from -1.5 to 1.5
- pattern: int32 [96, 96], P('rows', 'cols'), may hold values 0 or 1
- pivot_inverse: bfloat16 [2, 256, 256], replicated, may hold values from -0.375 to 0.375
- right_sides: float32 [96, 3, 256], P('rows'), may hold values from -6 to 6
Outputs:
- factored: bfloat16 [96, 96, 256, 256], P('rows', 'cols')
- forward: float32 [96, 3, 256], P('rows')
All inputs are finite; a program needn't handle non-finite values. No bound on the sum of `pattern` on one device may be relied on, other than what follows from the above.
Results may differ from a plain program's by a relative error of at most 0.0071.
Values may be sent and summed in bfloat16 or wider, within the bound.
A program may use at most 128 MiB of HBM per device.

v0:
```python
import jax
import jax.numpy as jnp
from jax import lax
from jax.sharding import PartitionSpec as P


def spread(x, axis, root):
    mine = lax.axis_index(axis) == root
    return lax.psum(jnp.where(mine, x, jnp.zeros_like(x)), axis)


def schur(part, lower, upper, live_part):
    prod = jnp.einsum("iab,jbc->ijac", lower, upper, preferred_element_type=jnp.float32)
    fresh = (part.astype(jnp.float32) - prod).astype(jnp.bfloat16)
    return jnp.where(live_part[:, :, None, None], fresh, part)


def on_device(blocks, pattern, pivot_inverse, right_sides):
    row_count = blocks.shape[0]
    nrows = lax.axis_size("rows")
    ncols = lax.axis_size("cols")
    row_glob = jnp.arange(row_count) * nrows + lax.axis_index("rows")
    col_glob = jnp.arange(blocks.shape[1]) * ncols + lax.axis_index("cols")
    live = pattern == 1
    zero_block = jnp.zeros((), jnp.bfloat16)
    matrix = jnp.where(live[:, :, None, None], blocks, zero_block)

    def column_panel(column, step):
        scaled = jnp.einsum(
            "nab,bc->nac", column, pivot_inverse[step], preferred_element_type=jnp.float32
        ).astype(jnp.bfloat16)
        landed = spread(scaled, "cols", step % ncols)
        return jnp.where((row_glob > step)[:, None, None], landed, zero_block)

    def pivot_panel(rowblocks, step):
        landed = spread(rowblocks, "rows", step % nrows)
        return jnp.where((col_glob > step)[:, None, None], landed, zero_block)

    def place_lower(matrix, lower, step):
        where_lower = (col_glob == step)[None, :] & (row_glob > step)[:, None]
        return jnp.where(where_lower[:, :, None, None], lower[:, None], matrix)

    lower_zero = column_panel(matrix[:, 0], 0)
    upper_zero = pivot_panel(matrix[0], 0)
    matrix = schur(matrix, lower_zero, upper_zero, live)
    lower_one = column_panel(matrix[:, 0], 1)
    upper_one = pivot_panel(matrix[0], 1)
    matrix = place_lower(matrix, lower_zero, 0)
    matrix = schur(matrix, lower_one, upper_one, live)
    matrix = place_lower(matrix, lower_one, 1)
    first = spread(right_sides[0], "rows", 0)
    rhs = right_sides - jnp.einsum(
        "nab,cb->nca", lower_zero.astype(jnp.float32), first, precision=lax.Precision.HIGHEST
    )
    second = spread(rhs[1 // nrows], "rows", 1 % nrows)
    rhs = rhs - jnp.einsum(
        "nab,cb->nca", lower_one.astype(jnp.float32), second, precision=lax.Precision.HIGHEST
    )
    return (matrix, rhs)


def solution(mesh):
    return jax.shard_map(
        on_device,
        mesh=mesh,
        in_specs=(P("rows", "cols", None, None), P("rows", "cols"), P(), P("rows", None, None)),
        out_specs=(P("rows", "cols", None, None), P("rows", None, None)),
        check_vma=False,
    )
```

profile of v0, /device:TPU:0, one launch (start us, length us, event | category | flops | bytes accessed | tf_op | source)
XLA Modules:
  0.0 362.8 jit_solution(4188063975407825787)
XLA Ops:
  7.2 0.7 broadcast_compare_fusion
  7.9 8.2 %copy_select_fusion = bf16[12,6,256,256]{3,2,0,1:T(8,128)(2,1)} fusion(bf16[12,6,256,256]{3,2,1,0:T(8,128)(2,1)} %param.4, pred[12,6]{0,1:T(8,128)(4,1)S(1)} %broadcast_compare_fusion), kind=kLoop, calls=%fused_computation.7 | loop fusion | flops 4718592 | bytes 18874440 | tf_op jit(solution)/shard_map/jit(_where)/select_n | solution.py:26
  16.1 3.1 broadcast_select_fusion.2
  19.2 0.0 all-reduce.5.cloned.1.call-start
  19.3 2.1 fusion.11
  21.4 0.0 all-reduce.9.cloned.1.call-start
  21.5 89.4 %all-reduce.7.cloned.1.call-done = bf16[12,256,256]{2,1,0:T(8,128)(2,1)} async-done(((bf16[12,256,256]{2,1,0:T(8,128)(2,1)}), bf16[12,256,256]{2,1,0:T(8,128)(2,1)}) %all-reduce.7.cloned.1.call-update) | async-done | bytes 1572880 | tf_op jit(solution)/shard_map/psum | solution.py:9
  110.9 1.6 broadcast_select_fusion
  112.5 62.1 %all-reduce.5.cloned.1.call-done = bf16[6,256,256]{2,1,0:T(8,128)(2,1)} async-done(((bf16[6,256,256]{2,1,0:T(8,128)(2,1)}), bf16[6,256,256]{2,1,0:T(8,128)(2,1)}) %all-reduce.5.cloned.1.call-update) | async-done | bytes 786448 | tf_op jit(solution)/shard_map/psum | solution.py:9
  174.6 6.5 %fusion.2 = bf16[12,6,256,256]{3,2,0,1:T(8,128)(2,1)S(1)} fusion(pred[12,6]{0,1:T(8,128)(4,1)S(1)} %broadcast_compare_fusion, bf16[12,256,256]{2,1,0:T(8,128)(2,1)S(1)} %broadcast_select_fusion, bf16[6,256,256]{2,1,0:T(8,128)(2,1)} %all-reduce.5.cloned.1.call-done, pred[6]{0:T(512)(128)(4,1)S(1)} %broadcast_compare_fusion.2, bf16[12,6,256,256]{3,2,1,0:T(8,128)(2,1)} %param.4), kind=kOutput, calls=%fused_computation.4 | convolution fusion | flops 2439905280 | bytes 21233742 | tf_op jit(solution)/shard_map/iab,jbc->ijac/dot_general | solution.py:13
  181.0 3.7 %copy-done = bf16[12,6,256,256]{3,2,0,1:T(8,128)(2,1)} copy-done((bf16[12,6,256,256]{3,2,0,1:T(8,128)(2,1)}, bf16[12,6,256,256]{3,2,0,1:T(8,128)(2,1)S(1)}, u32[]{:S(2)}) %copy-start) | copy-done | bytes 9437208
  184.8 1.7 broadcast_select_fusion.3
  186.6 13.4 %psum.46 = f32[3,256]{1,0:T(4,128)S(1)} all-reduce(f32[3,256]{1,0:T(4,128)S(1)} %select_bitcast_fusion), channel_id=1, replica_groups=mesh['rows'=8,'cols'=16] {'rows'}, use_global_device_ids=true, to_apply=%region_4.5 | all-reduce | flops 768 | bytes 6144 | tf_op jit(solution)/shard_map/psum | solution.py:9
  200.0 0.1 broadcast_and_fusion
  200.1 0.1 broadcast_and_fusion.1
  200.1 1.3 fusion.8
  201.4 12.7 %psum.47 = f32[3,256]{1,0:T(4,128)S(1)} all-reduce(f32[3,256]{1,0:T(4,128)S(1)} %fusion.24), channel_id=1, replica_groups=mesh['rows'=8,'cols'=16] {'rows'}, use_global_device_ids=true, to_apply=%region_5.6 | all-reduce | flops 768 | bytes 6144 | tf_op jit(solution)/shard_map/psum | solution.py:9
  214.1 2.1 fusion.9
  216.2 58.7 %all-reduce.9.cloned.1.call-done = bf16[12,256,256]{2,1,0:T(8,128)(2,1)} async-done(((bf16[12,256,256]{2,1,0:T(8,128)(2,1)}), bf16[12,256,256]{2,1,0:T(8,128)(2,1)}) %all-reduce.9.cloned.1.call-update) | async-done | bytes 1572880 | tf_op jit(solution)/shard_map/psum | solution.py:9
  274.9 1.6 broadcast_select_fusion.1
  276.5 2.0 fusion.7
  278.5 59.9 %all-reduce.11.cloned.1.call-done = bf16[6,256,256]{2,1,0:T(8,128)(2,1)} async-done(((bf16[6,256,256]{2,1,0:T(8,128)(2,1)}), bf16[6,256,256]{2,1,0:T(8,128)(2,1)}) %all-reduce.11.cloned.1.call-update) | async-done | bytes 786448 | tf_op jit(solution)/shard_map/psum | solution.py:9
  338.4 9.3 %fusion.4 = bf16[12,6,256,256]{3,2,0,1:T(8,128)(2,1)} fusion(bf16[12,6,256,256]{3,2,0,1:T(8,128)(2,1)} %copy-done, pred[12,6]{0,1:T(8,128)(4,1)S(1)} %broadcast_and_fusion, pred[12,6]{0,1:T(8,128)(4,1)S(1)} %broadcast_compare_fusion, pred[12,6]{0,1:T(8,128)(4,1)S(1)} %broadcast_and_fusion.1, bf16[12,256,256]{2,1,0:T(8,128)(2,1)S(1)} %broadcast_select_fusion, ...), kind=kOutput, calls=%fused_computation.6 | convolution fusion | flops 2444623872 | bytes 22806750 | tf_op jit(solution)/shard_map/iab,jbc->ijac/dot_general | solution.py:13
  347.8 8.6 %copy.13 = bf16[12,6,256,256]{3,2,1,0:T(8,128)(2,1)} copy(bf16[12,6,256,256]{3,2,0,1:T(8,128)(2,1)} %fusion.4) | data formatting | bytes 18874368
  (18 shorter events, 0.2 us)
Async XLA Ops:
  7.2 103.7 %all-reduce.7.cloned.1.call-start = ((), (), s32[]{:S(2)}) async-start(), calls=%async_computation.1 | async-start | bytes 3145728 | tf_op jit(solution)/shard_map/psum | solution.py:9
  7.9 8.2 %copy-start.2 = (bf16[2,256,256]{2,1,0:T(8,128)(2,1)S(1)}, bf16[2,256,256]{2,1,0:T(8,128)(2,1)}, u32[]{:S(2)}) copy-start(bf16[2,256,256]{2,1,0:T(8,128)(2,1)} %param.6) | copy-start | bytes 786436
  19.2 155.3 %all-reduce.5.cloned.1.call-start = ((), (), s32[]{:S(2)}) async-start(), calls=%async_computation | async-start | bytes 1572864 | tf_op jit(solution)/shard_map/psum | solution.py:9
  21.4 253.5 %all-reduce.9.cloned.1.call-start = ((), (), s32[]{:S(2)}) async-start(), calls=%async_computation.2 | async-start | bytes 3145728 | tf_op jit(solution)/shard_map/psum | solution.py:9
  181.0 3.7 %copy-start = (bf16[12,6,256,256]{3,2,0,1:T(8,128)(2,1)}, bf16[12,6,256,256]{3,2,0,1:T(8,128)(2,1)S(1)}, u32[]{:S(2)}) copy-start(bf16[12,6,256,256]{3,2,0,1:T(8,128)(2,1)S(1)} %fusion.2) | copy-start | bytes 28311556
  184.8 1.8 copy-start.1
  186.5 151.9 %all-reduce.11.cloned.1.call-start = ((), (), s32[]{:S(2)}) async-start(), calls=%async_computation.3 | async-start | bytes 1572864 | tf_op jit(solution)/shard_map/psum | solution.py:9
Sparse Core Ops, SparseCore 0:
  19.4 91.4 all-reduce.6
  113.2 61.2 all-reduce.4
  186.6 88.2 all-reduce.8
  277.1 61.2 all-reduce.10
where the time goes:
time: 363 us
  waiting for transfers between devices  270 us (74%)
  blocking collectives  26 us (7%)
  matrix products  23.9 us (7%)
  other arithmetic  16.4 us (5%)
  between operations  13.9 us (4%)
  local copies, waits for them, and re-layouts  12.3 us (3%)
    psum x4, waiting for transfers between devices, spread(): return lax.psum(jnp.where(mine, x, jnp.zeros_like(x)), axis)  270 us
    psum x2, blocking collectives, spread(): return lax.psum(jnp.where(mine, x, jnp.zeros_like(x)), axis)  26 us
    dot_general x2, matrix products, schur(): jnp.einsum('iab,jbc->ijac', lower, upper, preferred_element_type=jnp.floa...  15.8 us
    unnamed x7, local copies, waits for them, and re-layouts  12.3 us
    select_n x1, other arithmetic, on_device(): matrix = jnp.where(live[:, :, None, None], blocks, zero_block)  8.17 us
  transfers between devices with their start and end apart: 4, of which 4 were waited for; matrix products, arithmetic and copies ran while one was open for 3% of the time, Pallas kernels for 0%

commit v1 on v0

--- a/solution.py
+++ b/solution.py
@@ -6,7 +6,7 @@
 
 def spread(x, axis, root):
     mine = lax.axis_index(axis) == root
-    return lax.psum(jnp.where(mine, x, jnp.zeros_like(x)), axis)
+    return jnp.sum(lax.all_gather(jnp.where(mine, x, jnp.zeros_like(x)), axis), axis=0)
 
 
 def schur(part, lower, upper, live_part):

time: 363 us -> 480 us (1.32)
  waiting for transfers between devices: 270 us -> 353 us
  other arithmetic: 16.4 us -> 48.3 us
    all_gather x0 -> x4, waiting for transfers between devices: none -> 353 us  [spread(): lax.all_gather(jnp.where(mine, x, jnp.zeros_like(x)), axis)]
    psum x4 -> x0, waiting for transfers between devices: 270 us -> none  [spread(): return lax.psum(jnp.where(mine, x, jnp.zeros_like(x)), axis)]
    reduce_sum x0 -> x6, other arithmetic: none -> 35.9 us  [spread(): jnp.sum(lax.all_gather(jnp.where(mine, x, jnp.zeros_like(x)), axis), axis=0)]
    all_gather x0 -> x2, blocking collectives: none -> 26.6 us  [spread(): lax.all_gather(jnp.where(mine, x, jnp.zeros_like(x)), axis)]
    psum x2 -> x0, blocking collectives: 26 us -> none  [spread(): return lax.psum(jnp.where(mine, x, jnp.zeros_like(x)), axis)]
    unnamed x7 -> x9, local copies, waits for them, and re-layouts: 12.3 us -> 12.3 us
  transfers between devices with their start and end apart: 4 -> 4, of which waited for: 4 -> 4; matrix products, arithmetic and copies ran while one was open for 3% -> 4% of each run, Pallas kernels for 0% -> 0%
where the time goes in v1:
time: 480 us; the launch traced here: 479 us
  waiting for transfers between devices  353 us (74%)
  other arithmetic  48.3 us (10%)
  blocking collectives  26.6 us (6%)
  matrix products  25.3 us (5%)
  between operations  13.9 us (3%)
  local copies, waits for them, and re-layouts  12.3 us (3%)
    all_gather x4, waiting for transfers between devices, spread(): lax.all_gather(jnp.where(mine, x, jnp.zeros_like(x)), axis)  353 us
    reduce_sum x6, other arithmetic, spread(): jnp.sum(lax.all_gather(jnp.where(mine, x, jnp.zeros_like(x)), axis), axis=0)  35.9 us
    all_gather x2, blocking collectives, spread(): lax.all_gather(jnp.where(mine, x, jnp.zeros_like(x)), axis)  26.6 us
    dot_general x2, matrix products, schur(): jnp.einsum('iab,jbc->ijac', lower, upper, preferred_element_type=jnp.floa...  15.7 us
    unnamed x9, local copies, waits for them, and re-layouts  12.3 us
  transfers between devices with their start and end apart: 4, of which 4 were waited for; matrix products, arithmetic and copies ran while one was open for 4% of the time, Pallas kernels for 0%

profile of v1, /device:TPU:0, one launch (start us, length us, event | category | flops | bytes accessed | tf_op | source)
XLA Modules:
  0.0 479.2 jit_solution(6340565999700283684)
XLA Ops:
  7.2 0.7 broadcast_compare_fusion
  7.9 8.2 %copy_select_fusion = bf16[12,6,256,256]{3,2,0,1:T(8,128)(2,1)} fusion(bf16[12,6,256,256]{3,2,1,0:T(8,128)(2,1)} %param.4, pred[12,6]{0,1:T(8,128)(4,1)S(1)} %broadcast_compare_fusion), kind=kLoop, calls=%fused_computation.7 | loop fusion | flops 4718592 | bytes 18874440 | tf_op jit(solution)/shard_map/jit(_where)/select_n | solution.py:26
  16.1 2.1 slice_select_fusion.1
  18.3 3.2 broadcast_select_fusion.2
  21.5 40.1 %all-gather.7.cloned.1.call-done = bf16[8,6,256,256]{3,2,0,1:T(8,128)(2,1)} async-done(((bf16[1,6,256,256]{3,2,0,1:T(8,128)(2,1)}), bf16[8,6,256,256]{3,2,0,1:T(8,128)(2,1)}) %all-gather.7.cloned.1.call-update) | async-done | bytes 6291472 | tf_op jit(solution)/shard_map/all_gather | solution.py:9
  61.6 4.8 %reduce_sum.66 = bf16[6,256,256]{2,1,0:T(8,128)(2,1)} reduce(bf16[8,6,256,256]{3,2,0,1:T(8,128)(2,1)} %all-gather.7.cloned.1.call-done, bf16[]{:T(256)} %constant.15.clone.1), dimensions={0}, to_apply=%region_0.1 | reduce | flops 2752512 | bytes 7077890 | tf_op jit(solution)/shard_map/reduce_sum | solution.py:9
  66.5 151.7 %all-gather.11.cloned.1.call-done = bf16[192,256,256]{2,1,0:T(8,128)(2,1)} async-done(((bf16[12,256,256]{2,1,0:T(8,128)(2,1)}), bf16[192,256,256]{2,1,0:T(8,128)(2,1)}) %all-gather.11.cloned.1.call-update) | async-done | bytes 25165840 | tf_op jit(solution)/shard_map/all_gather | solution.py:9
  218.1 13.1 %reduce_sum.67 = bf16[12,256,256]{2,1,0:T(8,128)(2,1)S(1)} reduce(bf16[16,12,256,256]{3,2,1,0:T(8,128)(2,1)} %bitcast.67, bf16[]{:T(256)} %constant.15.clone.1), dimensions={0}, to_apply=%region_1.2 | reduce | flops 11796480 | bytes 26738690 | tf_op jit(solution)/shard_map/reduce_sum | solution.py:9
  231.2 0.2 broadcast_select_fusion
  231.4 6.5 %fusion.2 = bf16[12,6,256,256]{3,2,0,1:T(8,128)(2,1)S(1)} fusion(pred[12,6]{0,1:T(8,128)(4,1)S(1)} %broadcast_compare_fusion, bf16[12,256,256]{2,1,0:T(8,128)(2,1)S(1)} %broadcast_select_fusion, bf16[6,256,256]{2,1,0:T(8,128)(2,1)} %reduce_sum.66, pred[6]{0:T(512)(128)(4,1)S(1)} %broadcast_compare_fusion.2, bf16[12,6,256,256]{3,2,1,0:T(8,128)(2,1)} %param.4), kind=kOutput, calls=%fused_computation.4 | convolution fusion | flops 2439905280 | bytes 21233742 | tf_op jit(solution)/shard_map/iab,jbc->ijac/dot_general | solution.py:13
  237.9 3.7 copy-done.1
  241.6 1.0 slice_select_fusion
  242.7 3.2 broadcast_select_fusion.3
  245.9 13.3 %all_gather.34 = f32[8,3,256]{2,1,0:T(4,128)S(1)} all-gather(f32[1,3,256]{2,1,0:T(4,128)S(1)} %slice_select_fusion.3), channel_id=1, replica_groups=mesh['rows'=8,'cols'=16] {'rows'}, dimensions={0}, use_global_device_ids=true | all-gather | bytes 27648 | tf_op jit(solution)/shard_map/all_gather | solution.py:9
  259.4 1.3 fusion.8
  260.7 13.3 %all_gather.35 = f32[8,3,256]{2,1,0:T(4,128)S(1)} all-gather(f32[1,3,256]{2,1,0:T(4,128)S(1)} %slice_select_fusion.2), channel_id=1, replica_groups=mesh['rows'=8,'cols'=16] {'rows'}, dimensions={0}, use_global_device_ids=true | all-gather | bytes 27648 | tf_op jit(solution)/shard_map/all_gather | solution.py:9
  274.0 9.3 %all-gather.9.cloned.1.call-done = bf16[8,6,256,256]{3,2,0,1:T(8,128)(2,1)} async-done(((bf16[1,6,256,256]{3,2,0,1:T(8,128)(2,1)}), bf16[8,6,256,256]{3,2,0,1:T(8,128)(2,1)}) %all-gather.9.cloned.1.call-update) | async-done | bytes 6291472 | tf_op jit(solution)/shard_map/all_gather | solution.py:9
  283.3 4.8 %reduce_sum.69 = bf16[6,256,256]{2,1,0:T(8,128)(2,1)} reduce(bf16[8,6,256,256]{3,2,0,1:T(8,128)(2,1)} %all-gather.9.cloned.1.call-done, bf16[]{:T(256)} %constant.15.clone.1), dimensions={0}, to_apply=%region_3.4 | reduce | flops 2752512 | bytes 7077890 | tf_op jit(solution)/shard_map/reduce_sum | solution.py:9
  288.2 151.5 %all-gather.13.cloned.1.call-done = bf16[192,256,256]{2,1,0:T(8,128)(2,1)} async-done(((bf16[12,256,256]{2,1,0:T(8,128)(2,1)}), bf16[192,256,256]{2,1,0:T(8,128)(2,1)}) %all-gather.13.cloned.1.call-update) | async-done | bytes 25165840 | tf_op jit(solution)/shard_map/all_gather | solution.py:9
  439.6 13.1 %reduce_sum.68 = bf16[12,256,256]{2,1,0:T(8,128)(2,1)S(1)} reduce(bf16[16,12,256,256]{3,2,1,0:T(8,128)(2,1)} %bitcast.66, bf16[]{:T(256)} %constant.15.clone.1), dimensions={0}, to_apply=%region_2.3 | reduce | flops 11796480 | bytes 26738690 | tf_op jit(solution)/shard_map/reduce_sum | solution.py:9
  452.7 0.2 broadcast_select_fusion.1
  452.9 2.0 fusion.7
  454.9 9.3 %fusion.4 = bf16[12,6,256,256]{3,2,0,1:T(8,128)(2,1)} fusion(bf16[12,6,256,256]{3,2,0,1:T(8,128)(2,1)} %copy-done.1, pred[12,6]{0,1:T(8,128)(4,1)S(1)} %broadcast_and_fusion, pred[12,6]{0,1:T(8,128)(4,1)S(1)} %broadcast_compare_fusion, pred[12,6]{0,1:T(8,128)(4,1)S(1)} %broadcast_and_fusion.1, bf16[12,256,256]{2,1,0:T(8,128)(2,1)S(1)} %broadcast_select_fusion, ...), kind=kOutput, calls=%fused_computation.6 | convolution fusion | flops 2444623872 | bytes 22806750 | tf_op jit(solution)/shard_map/iab,jbc->ijac/dot_general | solution.py:13
  464.1 8.6 %copy.15 = bf16[12,6,256,256]{3,2,1,0:T(8,128)(2,1)} copy(bf16[12,6,256,256]{3,2,0,1:T(8,128)(2,1)} %fusion.4) | data formatting | bytes 18874368
  (26 shorter events, 0.5 us)
Async XLA Ops:
  7.2 54.5 %all-gather.7.cloned.1.call-start = ((), (), s32[]{:S(2)}) async-start(), calls=%async_computation | async-start | bytes 7077888 | tf_op jit(solution)/shard_map/all_gather | solution.py:9
  7.9 10.3 %copy-start.3 = (bf16[2,256,256]{2,1,0:T(8,128)(2,1)S(1)}, bf16[2,256,256]{2,1,0:T(8,128)(2,1)}, u32[]{:S(2)}) copy-start(bf16[2,256,256]{2,1,0:T(8,128)(2,1)} %param.6) | copy-start | bytes 786436
  18.2 199.9 %all-gather.11.cloned.1.call-start = ((), (), s32[]{:S(2)}) async-start(), calls=%async_computation.2 | async-start | bytes 26738688 | tf_op jit(solution)/shard_map/all_gather | solution.py:9
  21.4 261.9 %all-gather.9.cloned.1.call-start = ((), (), s32[]{:S(2)}) async-start(), calls=%async_computation.1 | async-start | bytes 7077888 | tf_op jit(solution)/shard_map/all_gather | solution.py:9
  237.9 3.7 copy-start.1
  241.6 4.2 copy-start.2
  242.6 197.0 %all-gather.13.cloned.1.call-start = ((), (), s32[]{:S(2)}) async-start(), calls=%async_computation.3 | async-start | bytes 26738688 | tf_op jit(solution)/shard_map/all_gather | solution.py:9
  452.7 2.1 copy-start
Sparse Core Ops, SparseCore 0:
  18.3 43.2 all-gather.6
  63.8 154.3 all-gather.10
  242.7 40.5 all-gather.8
  285.3 154.2 all-gather.12
